TPU v7x, 512 devices: a whole 4x8x8 slice. The times are simulated.
512 devices in a mesh: team: 16 (over y, core), tm: 32 (over x, z).
Axes of the slice: x: 4, y: 8, z: 8, core: 2. Of those that a mesh axis runs over, the one named last changes fastest.
Arguments:
- transitions: float32 [16, 32, 512, 512], P('team', 'tm'), may hold values from -0.25 to 1.25
- states: float32 [16, 32, 64, 512], P('team', 'tm'), may hold values from -1 to 1
- cotangent: float32 [16, 32, 64, 512], P('team', 'tm'), may hold values from -2.4 to 2.4
- terminal: float32 [16, 64, 512], P('team'), may hold values from -6 to 6
- incidence: int32 [16, 32, 32, 2048], P('team', 'tm'), may hold values 0 or 1
- measured: float32 [16, 32, 64, 32], P('team', 'tm'), may hold values from -0.12 to 0.12
- obs_gain: float32 [16, 512], P('team'), may hold values from -6 to 6
Outputs:
- adjoint: float32 [16, 32, 64, 512], P('team', 'tm')
- grad_transitions: bfloat16 [16, 32, 512, 512], P('team', 'tm')
All inputs are finite; a program needn't handle non-finite values. No bound on the sum of `incidence` on one device may be relied on, other than what follows from the above.
Results may differ from a plain program's by a relative error of at most 0.001.
Values sent between devices are 32-bit elements; how exact they have to be, the bound alone decides.
No kernel may reach another device: no remote copies, remote signals or barrier semaphores. Data moves between devices by JAX's collectives and lax.ppermute only.
A program may use at most 64 MiB of HBM per device.

v0:
```python
import jax
import jax.numpy as jnp
from jax import lax
from jax.sharding import PartitionSpec as P

STATES = 16
TEAM_STATES = 512
COLS = 64
HIGHEST = lax.Precision.HIGHEST


def from_behind(block, axis, distance):
    devices = range(lax.axis_size(axis))
    route = [(i - distance, i) for i in devices if i - distance in devices]
    return lax.ppermute(block, axis, route)


def matmul(left, right):
    return jnp.dot(left, right, precision=HIGHEST)


def shards(transitions, states, cotangent, terminal, incidence, measured, obs_gain):
    step_count = transitions.shape[1]
    matrices = transitions[0]
    incident = incidence[0].astype(jnp.float32)
    partial_value = jnp.einsum("scr,srl->scl", measured[0], incident, precision=HIGHEST)
    landmark = lax.psum(partial_value, "team")
    injection = jnp.einsum("scl,srl->scr", landmark, incident, precision=HIGHEST)
    driven = cotangent[0] + jnp.repeat(injection, STATES, axis=2) * obs_gain[0][None, None, :]
    offset = jnp.zeros((COLS, TEAM_STATES), jnp.float32)
    moment = 0
    offset = matmul(offset, matrices[moment]) + driven[moment]
    is_last = lax.axis_index("tm") == lax.axis_size("tm") - 1
    start_cot = jnp.where(is_last, terminal[0], jnp.zeros_like(terminal[0]))

    def advance_steps(turn, carried):
        outgoing = carried
        outgoing = matmul(outgoing, matrices[0])
        outgoing = outgoing + offset
        return from_behind(outgoing, "tm", -1) + start_cot

    incoming = lax.fori_loop(0, lax.axis_size("tm") - 1, advance_steps, start_cot)
    running = incoming
    adjoint_list = [None] * step_count
    grad_list = [None] * step_count
    moment = 0
    grad_now = jnp.einsum("cn,cm->nm", running, states[0, moment], precision=HIGHEST)
    grad_list[moment] = grad_now.astype(jnp.bfloat16)
    running = matmul(running, matrices[moment]) + driven[moment]
    adjoint_list[moment] = running
    adjoint = jnp.stack(adjoint_list)[None]
    grad_transitions = jnp.stack(grad_list)[None]
    return (adjoint, grad_transitions)


def solution(mesh):
    placed = (
        P("team", "tm", None, None),
        P("team", "tm", None, None),
        P("team", "tm", None, None),
        P("team", None, None),
        P("team", "tm", None, None),
        P("team", "tm", None, None),
        P("team", None),
    )
    return jax.shard_map(
        shards,
        mesh=mesh,
        in_specs=placed,
        out_specs=(P("team", "tm", None, None), P("team", "tm", None, None)),
        check_vma=False,
    )
```

profile of v0, /device:TPU:30, one launch (start us, length us, event | category | flops | bytes accessed | tf_op | source)
XLA Modules:
  0.0 454.6 jit_solution(4725242785528667431)
XLA Ops:
  10.6 120.1 %all-reduce.2.cloned.1.call-done = f32[64,2048]{1,0:T(8,128)} async-done(((f32[64,2048]{1,0:T(8,128)}), f32[64,2048]{1,0:T(8,128)}) %all-reduce.2.cloned.1.call-update) | async-done | bytes 524304 | tf_op jit(solution)/shard_map/psum | solution.py:27
  134.0 310.5 %while.10 = (s32[]{:T(128)}, f32[64,512]{1,0:T(8,128)S(1)}, f32[1,1,512,512]{3,2,1,0:T(8,128)S(1)}, f32[64,512]{1,0:T(8,128)S(1)}, f32[64,512]{1,0:T(8,128)S(1)}, /*index=5*/s32[]{:T(128)}) while((s32[]{:T(128)}, f32[64,512]{1,0:T(8,128)S(1)}, f32[1,1,512,512]{3,2,1,0:T(8,128)S(1)}, f32[64,512]{1,0:T(8,128)S(1)}, f32[64,512]{1,0:T(8,128)S(1)}, ...), condition=%wide.region_2.3_spmd, body=%wide.region_1.2_spmd.sunk | while | flops 201392128 | bytes 2359405 | solution.py:42
  134.8 6.1 %collective-permute-start = (f32[64,512]{1,0:T(8,128)S(1)}, f32[64,512]{1,0:T(8,128)S(1)}, u32[]{:S(2)}, u32[]{:S(2)}) collective-permute-start(f32[64,512]{1,0:T(8,128)S(1)} %convolution_add_fusion.4), channel_id=1, source_target_pairs={{1,0},{2,1},{3,2},{4,3},{5,4},{6,5},{7,6},{8,7},{9,8},{10,9},{11,1... | collective-permute-start | bytes 393224 | tf_op jit(solution)/shard_map/while/body/eval_jaxpr/ppermute | solution.py:15
  140.9 3.8 collective-permute-done
  145.5 6.5 %collective-permute-start = (f32[64,512]{1,0:T(8,128)S(1)}, f32[64,512]{1,0:T(8,128)S(1)}, u32[]{:S(2)}, u32[]{:S(2)}) collective-permute-start(f32[64,512]{1,0:T(8,128)S(1)} %convolution_add_fusion.4), channel_id=1, source_target_pairs={{1,0},{2,1},{3,2},{4,3},{5,4},{6,5},{7,6},{8,7},{9,8},{10,9},{11,1... | collective-permute-start | bytes 393224 | tf_op jit(solution)/shard_map/while/body/eval_jaxpr/ppermute | solution.py:15
  152.0 3.0 collective-permute-done
  155.8 6.5 %collective-permute-start = (f32[64,512]{1,0:T(8,128)S(1)}, f32[64,512]{1,0:T(8,128)S(1)}, u32[]{:S(2)}, u32[]{:S(2)}) collective-permute-start(f32[64,512]{1,0:T(8,128)S(1)} %convolution_add_fusion.4), channel_id=1, source_target_pairs={{1,0},{2,1},{3,2},{4,3},{5,4},{6,5},{7,6},{8,7},{9,8},{10,9},{11,1... | collective-permute-start | bytes 393224 | tf_op jit(solution)/shard_map/while/body/eval_jaxpr/ppermute | solution.py:15
  162.3 2.5 collective-permute-done
  165.6 6.5 %collective-permute-start = (f32[64,512]{1,0:T(8,128)S(1)}, f32[64,512]{1,0:T(8,128)S(1)}, u32[]{:S(2)}, u32[]{:S(2)}) collective-permute-start(f32[64,512]{1,0:T(8,128)S(1)} %convolution_add_fusion.4), channel_id=1, source_target_pairs={{1,0},{2,1},{3,2},{4,3},{5,4},{6,5},{7,6},{8,7},{9,8},{10,9},{11,1... | collective-permute-start | bytes 393224 | tf_op jit(solution)/shard_map/while/body/eval_jaxpr/ppermute | solution.py:15
  175.3 6.5 %collective-permute-start = (f32[64,512]{1,0:T(8,128)S(1)}, f32[64,512]{1,0:T(8,128)S(1)}, u32[]{:S(2)}, u32[]{:S(2)}) collective-permute-start(f32[64,512]{1,0:T(8,128)S(1)} %convolution_add_fusion.4), channel_id=1, source_target_pairs={{1,0},{2,1},{3,2},{4,3},{5,4},{6,5},{7,6},{8,7},{9,8},{10,9},{11,1... | collective-permute-start | bytes 393224 | tf_op jit(solution)/shard_map/while/body/eval_jaxpr/ppermute | solution.py:15
  181.8 2.5 collective-permute-done
  185.1 6.5 %collective-permute-start = (f32[64,512]{1,0:T(8,128)S(1)}, f32[64,512]{1,0:T(8,128)S(1)}, u32[]{:S(2)}, u32[]{:S(2)}) collective-permute-start(f32[64,512]{1,0:T(8,128)S(1)} %convolution_add_fusion.4), channel_id=1, source_target_pairs={{1,0},{2,1},{3,2},{4,3},{5,4},{6,5},{7,6},{8,7},{9,8},{10,9},{11,1... | collective-permute-start | bytes 393224 | tf_op jit(solution)/shard_map/while/body/eval_jaxpr/ppermute | solution.py:15
  194.8 6.5 %collective-permute-start = (f32[64,512]{1,0:T(8,128)S(1)}, f32[64,512]{1,0:T(8,128)S(1)}, u32[]{:S(2)}, u32[]{:S(2)}) collective-permute-start(f32[64,512]{1,0:T(8,128)S(1)} %convolution_add_fusion.4), channel_id=1, source_target_pairs={{1,0},{2,1},{3,2},{4,3},{5,4},{6,5},{7,6},{8,7},{9,8},{10,9},{11,1... | collective-permute-start | bytes 393224 | tf_op jit(solution)/shard_map/while/body/eval_jaxpr/ppermute | solution.py:15
  204.6 6.5 %collective-permute-start = (f32[64,512]{1,0:T(8,128)S(1)}, f32[64,512]{1,0:T(8,128)S(1)}, u32[]{:S(2)}, u32[]{:S(2)}) collective-permute-start(f32[64,512]{1,0:T(8,128)S(1)} %convolution_add_fusion.4), channel_id=1, source_target_pairs={{1,0},{2,1},{3,2},{4,3},{5,4},{6,5},{7,6},{8,7},{9,8},{10,9},{11,1... | collective-permute-start | bytes 393224 | tf_op jit(solution)/shard_map/while/body/eval_jaxpr/ppermute | solution.py:15
  211.1 2.8 collective-permute-done
  214.6 6.5 %collective-permute-start = (f32[64,512]{1,0:T(8,128)S(1)}, f32[64,512]{1,0:T(8,128)S(1)}, u32[]{:S(2)}, u32[]{:S(2)}) collective-permute-start(f32[64,512]{1,0:T(8,128)S(1)} %convolution_add_fusion.4), channel_id=1, source_target_pairs={{1,0},{2,1},{3,2},{4,3},{5,4},{6,5},{7,6},{8,7},{9,8},{10,9},{11,1... | collective-permute-start | bytes 393224 | tf_op jit(solution)/shard_map/while/body/eval_jaxpr/ppermute | solution.py:15
  221.1 3.8 collective-permute-done
  225.8 6.5 %collective-permute-start = (f32[64,512]{1,0:T(8,128)S(1)}, f32[64,512]{1,0:T(8,128)S(1)}, u32[]{:S(2)}, u32[]{:S(2)}) collective-permute-start(f32[64,512]{1,0:T(8,128)S(1)} %convolution_add_fusion.4), channel_id=1, source_target_pairs={{1,0},{2,1},{3,2},{4,3},{5,4},{6,5},{7,6},{8,7},{9,8},{10,9},{11,1... | collective-permute-start | bytes 393224 | tf_op jit(solution)/shard_map/while/body/eval_jaxpr/ppermute | solution.py:15
  232.2 3.0 collective-permute-done
  236.0 6.5 %collective-permute-start = (f32[64,512]{1,0:T(8,128)S(1)}, f32[64,512]{1,0:T(8,128)S(1)}, u32[]{:S(2)}, u32[]{:S(2)}) collective-permute-start(f32[64,512]{1,0:T(8,128)S(1)} %convolution_add_fusion.4), channel_id=1, source_target_pairs={{1,0},{2,1},{3,2},{4,3},{5,4},{6,5},{7,6},{8,7},{9,8},{10,9},{11,1... | collective-permute-start | bytes 393224 | tf_op jit(solution)/shard_map/while/body/eval_jaxpr/ppermute | solution.py:15
  242.5 2.5 collective-permute-done
  245.8 6.5 %collective-permute-start = (f32[64,512]{1,0:T(8,128)S(1)}, f32[64,512]{1,0:T(8,128)S(1)}, u32[]{:S(2)}, u32[]{:S(2)}) collective-permute-start(f32[64,512]{1,0:T(8,128)S(1)} %convolution_add_fusion.4), channel_id=1, source_target_pairs={{1,0},{2,1},{3,2},{4,3},{5,4},{6,5},{7,6},{8,7},{9,8},{10,9},{11,1... | collective-permute-start | bytes 393224 | tf_op jit(solution)/shard_map/while/body/eval_jaxpr/ppermute | solution.py:15
  252.2 2.5 collective-permute-done
  255.5 6.5 %collective-permute-start = (f32[64,512]{1,0:T(8,128)S(1)}, f32[64,512]{1,0:T(8,128)S(1)}, u32[]{:S(2)}, u32[]{:S(2)}) collective-permute-start(f32[64,512]{1,0:T(8,128)S(1)} %convolution_add_fusion.4), channel_id=1, source_target_pairs={{1,0},{2,1},{3,2},{4,3},{5,4},{6,5},{7,6},{8,7},{9,8},{10,9},{11,1... | collective-permute-start | bytes 393224 | tf_op jit(solution)/shard_map/while/body/eval_jaxpr/ppermute | solution.py:15
  265.3 6.5 %collective-permute-start = (f32[64,512]{1,0:T(8,128)S(1)}, f32[64,512]{1,0:T(8,128)S(1)}, u32[]{:S(2)}, u32[]{:S(2)}) collective-permute-start(f32[64,512]{1,0:T(8,128)S(1)} %convolution_add_fusion.4), channel_id=1, source_target_pairs={{1,0},{2,1},{3,2},{4,3},{5,4},{6,5},{7,6},{8,7},{9,8},{10,9},{11,1... | collective-permute-start | bytes 393224 | tf_op jit(solution)/shard_map/while/body/eval_jaxpr/ppermute | solution.py:15
  275.1 6.5 %collective-permute-start = (f32[64,512]{1,0:T(8,128)S(1)}, f32[64,512]{1,0:T(8,128)S(1)}, u32[]{:S(2)}, u32[]{:S(2)}) collective-permute-start(f32[64,512]{1,0:T(8,128)S(1)} %convolution_add_fusion.4), channel_id=1, source_target_pairs={{1,0},{2,1},{3,2},{4,3},{5,4},{6,5},{7,6},{8,7},{9,8},{10,9},{11,1... | collective-permute-start | bytes 393224 | tf_op jit(solution)/shard_map/while/body/eval_jaxpr/ppermute | solution.py:15
  284.8 6.5 %collective-permute-start = (f32[64,512]{1,0:T(8,128)S(1)}, f32[64,512]{1,0:T(8,128)S(1)}, u32[]{:S(2)}, u32[]{:S(2)}) collective-permute-start(f32[64,512]{1,0:T(8,128)S(1)} %convolution_add_fusion.4), channel_id=1, source_target_pairs={{1,0},{2,1},{3,2},{4,3},{5,4},{6,5},{7,6},{8,7},{9,8},{10,9},{11,1... | collective-permute-start | bytes 393224 | tf_op jit(solution)/shard_map/while/body/eval_jaxpr/ppermute | solution.py:15
  291.3 2.8 collective-permute-done
  294.8 6.5 %collective-permute-start = (f32[64,512]{1,0:T(8,128)S(1)}, f32[64,512]{1,0:T(8,128)S(1)}, u32[]{:S(2)}, u32[]{:S(2)}) collective-permute-start(f32[64,512]{1,0:T(8,128)S(1)} %convolution_add_fusion.4), channel_id=1, source_target_pairs={{1,0},{2,1},{3,2},{4,3},{5,4},{6,5},{7,6},{8,7},{9,8},{10,9},{11,1... | collective-permute-start | bytes 393224 | tf_op jit(solution)/shard_map/while/body/eval_jaxpr/ppermute | solution.py:15
  301.3 3.8 collective-permute-done
  306.0 6.5 %collective-permute-start = (f32[64,512]{1,0:T(8,128)S(1)}, f32[64,512]{1,0:T(8,128)S(1)}, u32[]{:S(2)}, u32[]{:S(2)}) collective-permute-start(f32[64,512]{1,0:T(8,128)S(1)} %convolution_add_fusion.4), channel_id=1, source_target_pairs={{1,0},{2,1},{3,2},{4,3},{5,4},{6,5},{7,6},{8,7},{9,8},{10,9},{11,1... | collective-permute-start | bytes 393224 | tf_op jit(solution)/shard_map/while/body/eval_jaxpr/ppermute | solution.py:15
  312.5 3.0 collective-permute-done
  316.2 6.5 %collective-permute-start = (f32[64,512]{1,0:T(8,128)S(1)}, f32[64,512]{1,0:T(8,128)S(1)}, u32[]{:S(2)}, u32[]{:S(2)}) collective-permute-start(f32[64,512]{1,0:T(8,128)S(1)} %convolution_add_fusion.4), channel_id=1, source_target_pairs={{1,0},{2,1},{3,2},{4,3},{5,4},{6,5},{7,6},{8,7},{9,8},{10,9},{11,1... | collective-permute-start | bytes 393224 | tf_op jit(solution)/shard_map/while/body/eval_jaxpr/ppermute | solution.py:15
  326.0 6.5 %collective-permute-start = (f32[64,512]{1,0:T(8,128)S(1)}, f32[64,512]{1,0:T(8,128)S(1)}, u32[]{:S(2)}, u32[]{:S(2)}) collective-permute-start(f32[64,512]{1,0:T(8,128)S(1)} %convolution_add_fusion.4), channel_id=1, source_target_pairs={{1,0},{2,1},{3,2},{4,3},{5,4},{6,5},{7,6},{8,7},{9,8},{10,9},{11,1... | collective-permute-start | bytes 393224 | tf_op jit(solution)/shard_map/while/body/eval_jaxpr/ppermute | solution.py:15
  335.8 6.5 %collective-permute-start = (f32[64,512]{1,0:T(8,128)S(1)}, f32[64,512]{1,0:T(8,128)S(1)}, u32[]{:S(2)}, u32[]{:S(2)}) collective-permute-start(f32[64,512]{1,0:T(8,128)S(1)} %convolution_add_fusion.4), channel_id=1, source_target_pairs={{1,0},{2,1},{3,2},{4,3},{5,4},{6,5},{7,6},{8,7},{9,8},{10,9},{11,1... | collective-permute-start | bytes 393224 | tf_op jit(solution)/shard_map/while/body/eval_jaxpr/ppermute | solution.py:15
  345.5 6.5 %collective-permute-start = (f32[64,512]{1,0:T(8,128)S(1)}, f32[64,512]{1,0:T(8,128)S(1)}, u32[]{:S(2)}, u32[]{:S(2)}) collective-permute-start(f32[64,512]{1,0:T(8,128)S(1)} %convolution_add_fusion.4), channel_id=1, source_target_pairs={{1,0},{2,1},{3,2},{4,3},{5,4},{6,5},{7,6},{8,7},{9,8},{10,9},{11,1... | collective-permute-start | bytes 393224 | tf_op jit(solution)/shard_map/while/body/eval_jaxpr/ppermute | solution.py:15
  355.3 6.5 %collective-permute-start = (f32[64,512]{1,0:T(8,128)S(1)}, f32[64,512]{1,0:T(8,128)S(1)}, u32[]{:S(2)}, u32[]{:S(2)}) collective-permute-start(f32[64,512]{1,0:T(8,128)S(1)} %convolution_add_fusion.4), channel_id=1, source_target_pairs={{1,0},{2,1},{3,2},{4,3},{5,4},{6,5},{7,6},{8,7},{9,8},{10,9},{11,1... | collective-permute-start | bytes 393224 | tf_op jit(solution)/shard_map/while/body/eval_jaxpr/ppermute | solution.py:15
  365.0 6.5 %collective-permute-start = (f32[64,512]{1,0:T(8,128)S(1)}, f32[64,512]{1,0:T(8,128)S(1)}, u32[]{:S(2)}, u32[]{:S(2)}) collective-permute-start(f32[64,512]{1,0:T(8,128)S(1)} %convolution_add_fusion.4), channel_id=1, source_target_pairs={{1,0},{2,1},{3,2},{4,3},{5,4},{6,5},{7,6},{8,7},{9,8},{10,9},{11,1... | collective-permute-start | bytes 393224 | tf_op jit(solution)/shard_map/while/body/eval_jaxpr/ppermute | solution.py:15
  371.5 2.8 collective-permute-done
  375.1 6.5 %collective-permute-start = (f32[64,512]{1,0:T(8,128)S(1)}, f32[64,512]{1,0:T(8,128)S(1)}, u32[]{:S(2)}, u32[]{:S(2)}) collective-permute-start(f32[64,512]{1,0:T(8,128)S(1)} %convolution_add_fusion.4), channel_id=1, source_target_pairs={{1,0},{2,1},{3,2},{4,3},{5,4},{6,5},{7,6},{8,7},{9,8},{10,9},{11,1... | collective-permute-start | bytes 393224 | tf_op jit(solution)/shard_map/while/body/eval_jaxpr/ppermute | solution.py:15
  381.6 3.9 collective-permute-done
  386.2 6.5 %collective-permute-start = (f32[64,512]{1,0:T(8,128)S(1)}, f32[64,512]{1,0:T(8,128)S(1)}, u32[]{:S(2)}, u32[]{:S(2)}) collective-permute-start(f32[64,512]{1,0:T(8,128)S(1)} %convolution_add_fusion.4), channel_id=1, source_target_pairs={{1,0},{2,1},{3,2},{4,3},{5,4},{6,5},{7,6},{8,7},{9,8},{10,9},{11,1... | collective-permute-start | bytes 393224 | tf_op jit(solution)/shard_map/while/body/eval_jaxpr/ppermute | solution.py:15
  392.7 3.0 collective-permute-done
  396.4 6.5 %collective-permute-start = (f32[64,512]{1,0:T(8,128)S(1)}, f32[64,512]{1,0:T(8,128)S(1)}, u32[]{:S(2)}, u32[]{:S(2)}) collective-permute-start(f32[64,512]{1,0:T(8,128)S(1)} %convolution_add_fusion.4), channel_id=1, source_target_pairs={{1,0},{2,1},{3,2},{4,3},{5,4},{6,5},{7,6},{8,7},{9,8},{10,9},{11,1... | collective-permute-start | bytes 393224 | tf_op jit(solution)/shard_map/while/body/eval_jaxpr/ppermute | solution.py:15
  406.2 6.5 %collective-permute-start = (f32[64,512]{1,0:T(8,128)S(1)}, f32[64,512]{1,0:T(8,128)S(1)}, u32[]{:S(2)}, u32[]{:S(2)}) collective-permute-start(f32[64,512]{1,0:T(8,128)S(1)} %convolution_add_fusion.4), channel_id=1, source_target_pairs={{1,0},{2,1},{3,2},{4,3},{5,4},{6,5},{7,6},{8,7},{9,8},{10,9},{11,1... | collective-permute-start | bytes 393224 | tf_op jit(solution)/shard_map/while/body/eval_jaxpr/ppermute | solution.py:15
  416.0 6.5 %collective-permute-start = (f32[64,512]{1,0:T(8,128)S(1)}, f32[64,512]{1,0:T(8,128)S(1)}, u32[]{:S(2)}, u32[]{:S(2)}) collective-permute-start(f32[64,512]{1,0:T(8,128)S(1)} %convolution_add_fusion.4), channel_id=1, source_target_pairs={{1,0},{2,1},{3,2},{4,3},{5,4},{6,5},{7,6},{8,7},{9,8},{10,9},{11,1... | collective-permute-start | bytes 393224 | tf_op jit(solution)/shard_map/while/body/eval_jaxpr/ppermute | solution.py:15
  425.8 6.5 %collective-permute-start = (f32[64,512]{1,0:T(8,128)S(1)}, f32[64,512]{1,0:T(8,128)S(1)}, u32[]{:S(2)}, u32[]{:S(2)}) collective-permute-start(f32[64,512]{1,0:T(8,128)S(1)} %convolution_add_fusion.4), channel_id=1, source_target_pairs={{1,0},{2,1},{3,2},{4,3},{5,4},{6,5},{7,6},{8,7},{9,8},{10,9},{11,1... | collective-permute-start | bytes 393224 | tf_op jit(solution)/shard_map/while/body/eval_jaxpr/ppermute | solution.py:15
  435.5 6.5 %collective-permute-start = (f32[64,512]{1,0:T(8,128)S(1)}, f32[64,512]{1,0:T(8,128)S(1)}, u32[]{:S(2)}, u32[]{:S(2)}) collective-permute-start(f32[64,512]{1,0:T(8,128)S(1)} %convolution_add_fusion.4), channel_id=1, source_target_pairs={{1,0},{2,1},{3,2},{4,3},{5,4},{6,5},{7,6},{8,7},{9,8},{10,9},{11,1... | collective-permute-start | bytes 393224 | tf_op jit(solution)/shard_map/while/body/eval_jaxpr/ppermute | solution.py:15
  (101 shorter events, 73.8 us)
Async XLA Ops:
  7.2 438.8 %copy-start = (f32[1,1,64,512]{3,2,1,0:T(8,128)S(1)}, f32[1,1,64,512]{3,2,1,0:T(8,128)}, u32[]{:S(2)}) copy-start(f32[1,1,64,512]{3,2,1,0:T(8,128)} %param.10) | copy-start | bytes 393220
  7.2 123.5 %all-reduce.2.cloned.1.call-start = ((), (), s32[]{:S(2)}) async-start(), calls=%async_computation | async-start | bytes 1048576 | tf_op jit(solution)/shard_map/psum | solution.py:27
  9.6 0.9 copy-start.4
  9.6 121.1 %copy-start.2 = (s32[1,1,32,2048]{3,2,1,0:T(8,128)S(1)}, s32[1,1,32,2048]{3,2,1,0:T(8,128)}, u32[]{:S(2)}) copy-start(s32[1,1,32,2048]{3,2,1,0:T(8,128)} %param.13) | copy-start | bytes 786436
  9.7 122.8 %copy-start.1 = (f32[1,1,512,512]{3,2,1,0:T(8,128)S(1)}, f32[1,1,512,512]{3,2,1,0:T(8,128)}, u32[]{:S(2)}) copy-start(f32[1,1,512,512]{3,2,1,0:T(8,128)} %param.9) | copy-start | bytes 3145732
  132.3 0.9 copy-start.3
  132.4 0.9 copy-start.5
  134.8 10.0 %collective-permute-start = (f32[64,512]{1,0:T(8,128)S(1)}, f32[64,512]{1,0:T(8,128)S(1)}, u32[]{:S(2)}, u32[]{:S(2)}) collective-permute-start(f32[64,512]{1,0:T(8,128)S(1)} %convolution_add_fusion.4), channel_id=1, source_target_pairs={{1,0},{2,1},{3,2},{4,3},{5,4},{6,5},{7,6},{8,7},{9,8},{10,9},{11,1... | collective-permute-start | bytes 393224 | tf_op jit(solution)/shard_map/while/body/eval_jaxpr/ppermute | solution.py:15
  145.5 9.4 %collective-permute-start = (f32[64,512]{1,0:T(8,128)S(1)}, f32[64,512]{1,0:T(8,128)S(1)}, u32[]{:S(2)}, u32[]{:S(2)}) collective-permute-start(f32[64,512]{1,0:T(8,128)S(1)} %convolution_add_fusion.4), channel_id=1, source_target_pairs={{1,0},{2,1},{3,2},{4,3},{5,4},{6,5},{7,6},{8,7},{9,8},{10,9},{11,1... | collective-permute-start | bytes 393224 | tf_op jit(solution)/shard_map/while/body/eval_jaxpr/ppermute | solution.py:15
  155.8 9.0 %collective-permute-start = (f32[64,512]{1,0:T(8,128)S(1)}, f32[64,512]{1,0:T(8,128)S(1)}, u32[]{:S(2)}, u32[]{:S(2)}) collective-permute-start(f32[64,512]{1,0:T(8,128)S(1)} %convolution_add_fusion.4), channel_id=1, source_target_pairs={{1,0},{2,1},{3,2},{4,3},{5,4},{6,5},{7,6},{8,7},{9,8},{10,9},{11,1... | collective-permute-start | bytes 393224 | tf_op jit(solution)/shard_map/while/body/eval_jaxpr/ppermute | solution.py:15
  165.6 9.0 %collective-permute-start = (f32[64,512]{1,0:T(8,128)S(1)}, f32[64,512]{1,0:T(8,128)S(1)}, u32[]{:S(2)}, u32[]{:S(2)}) collective-permute-start(f32[64,512]{1,0:T(8,128)S(1)} %convolution_add_fusion.4), channel_id=1, source_target_pairs={{1,0},{2,1},{3,2},{4,3},{5,4},{6,5},{7,6},{8,7},{9,8},{10,9},{11,1... | collective-permute-start | bytes 393224 | tf_op jit(solution)/shard_map/while/body/eval_jaxpr/ppermute | solution.py:15
  175.3 9.0 %collective-permute-start = (f32[64,512]{1,0:T(8,128)S(1)}, f32[64,512]{1,0:T(8,128)S(1)}, u32[]{:S(2)}, u32[]{:S(2)}) collective-permute-start(f32[64,512]{1,0:T(8,128)S(1)} %convolution_add_fusion.4), channel_id=1, source_target_pairs={{1,0},{2,1},{3,2},{4,3},{5,4},{6,5},{7,6},{8,7},{9,8},{10,9},{11,1... | collective-permute-start | bytes 393224 | tf_op jit(solution)/shard_map/while/body/eval_jaxpr/ppermute | solution.py:15
  185.1 9.0 %collective-permute-start = (f32[64,512]{1,0:T(8,128)S(1)}, f32[64,512]{1,0:T(8,128)S(1)}, u32[]{:S(2)}, u32[]{:S(2)}) collective-permute-start(f32[64,512]{1,0:T(8,128)S(1)} %convolution_add_fusion.4), channel_id=1, source_target_pairs={{1,0},{2,1},{3,2},{4,3},{5,4},{6,5},{7,6},{8,7},{9,8},{10,9},{11,1... | collective-permute-start | bytes 393224 | tf_op jit(solution)/shard_map/while/body/eval_jaxpr/ppermute | solution.py:15
  194.8 9.0 %collective-permute-start = (f32[64,512]{1,0:T(8,128)S(1)}, f32[64,512]{1,0:T(8,128)S(1)}, u32[]{:S(2)}, u32[]{:S(2)}) collective-permute-start(f32[64,512]{1,0:T(8,128)S(1)} %convolution_add_fusion.4), channel_id=1, source_target_pairs={{1,0},{2,1},{3,2},{4,3},{5,4},{6,5},{7,6},{8,7},{9,8},{10,9},{11,1... | collective-permute-start | bytes 393224 | tf_op jit(solution)/shard_map/while/body/eval_jaxpr/ppermute | solution.py:15
  204.6 9.2 %collective-permute-start = (f32[64,512]{1,0:T(8,128)S(1)}, f32[64,512]{1,0:T(8,128)S(1)}, u32[]{:S(2)}, u32[]{:S(2)}) collective-permute-start(f32[64,512]{1,0:T(8,128)S(1)} %convolution_add_fusion.4), channel_id=1, source_target_pairs={{1,0},{2,1},{3,2},{4,3},{5,4},{6,5},{7,6},{8,7},{9,8},{10,9},{11,1... | collective-permute-start | bytes 393224 | tf_op jit(solution)/shard_map/while/body/eval_jaxpr/ppermute | solution.py:15
  214.6 10.4 %collective-permute-start = (f32[64,512]{1,0:T(8,128)S(1)}, f32[64,512]{1,0:T(8,128)S(1)}, u32[]{:S(2)}, u32[]{:S(2)}) collective-permute-start(f32[64,512]{1,0:T(8,128)S(1)} %convolution_add_fusion.4), channel_id=1, source_target_pairs={{1,0},{2,1},{3,2},{4,3},{5,4},{6,5},{7,6},{8,7},{9,8},{10,9},{11,1... | collective-permute-start | bytes 393224 | tf_op jit(solution)/shard_map/while/body/eval_jaxpr/ppermute | solution.py:15
  225.8 9.4 %collective-permute-start = (f32[64,512]{1,0:T(8,128)S(1)}, f32[64,512]{1,0:T(8,128)S(1)}, u32[]{:S(2)}, u32[]{:S(2)}) collective-permute-start(f32[64,512]{1,0:T(8,128)S(1)} %convolution_add_fusion.4), channel_id=1, source_target_pairs={{1,0},{2,1},{3,2},{4,3},{5,4},{6,5},{7,6},{8,7},{9,8},{10,9},{11,1... | collective-permute-start | bytes 393224 | tf_op jit(solution)/shard_map/while/body/eval_jaxpr/ppermute | solution.py:15
  236.0 9.0 %collective-permute-start = (f32[64,512]{1,0:T(8,128)S(1)}, f32[64,512]{1,0:T(8,128)S(1)}, u32[]{:S(2)}, u32[]{:S(2)}) collective-permute-start(f32[64,512]{1,0:T(8,128)S(1)} %convolution_add_fusion.4), channel_id=1, source_target_pairs={{1,0},{2,1},{3,2},{4,3},{5,4},{6,5},{7,6},{8,7},{9,8},{10,9},{11,1... | collective-permute-start | bytes 393224 | tf_op jit(solution)/shard_map/while/body/eval_jaxpr/ppermute | solution.py:15
  245.8 9.0 %collective-permute-start = (f32[64,512]{1,0:T(8,128)S(1)}, f32[64,512]{1,0:T(8,128)S(1)}, u32[]{:S(2)}, u32[]{:S(2)}) collective-permute-start(f32[64,512]{1,0:T(8,128)S(1)} %convolution_add_fusion.4), channel_id=1, source_target_pairs={{1,0},{2,1},{3,2},{4,3},{5,4},{6,5},{7,6},{8,7},{9,8},{10,9},{11,1... | collective-permute-start | bytes 393224 | tf_op jit(solution)/shard_map/while/body/eval_jaxpr/ppermute | solution.py:15
  255.5 9.0 %collective-permute-start = (f32[64,512]{1,0:T(8,128)S(1)}, f32[64,512]{1,0:T(8,128)S(1)}, u32[]{:S(2)}, u32[]{:S(2)}) collective-permute-start(f32[64,512]{1,0:T(8,128)S(1)} %convolution_add_fusion.4), channel_id=1, source_target_pairs={{1,0},{2,1},{3,2},{4,3},{5,4},{6,5},{7,6},{8,7},{9,8},{10,9},{11,1... | collective-permute-start | bytes 393224 | tf_op jit(solution)/shard_map/while/body/eval_jaxpr/ppermute | solution.py:15
  265.3 9.0 %collective-permute-start = (f32[64,512]{1,0:T(8,128)S(1)}, f32[64,512]{1,0:T(8,128)S(1)}, u32[]{:S(2)}, u32[]{:S(2)}) collective-permute-start(f32[64,512]{1,0:T(8,128)S(1)} %convolution_add_fusion.4), channel_id=1, source_target_pairs={{1,0},{2,1},{3,2},{4,3},{5,4},{6,5},{7,6},{8,7},{9,8},{10,9},{11,1... | collective-permute-start | bytes 393224 | tf_op jit(solution)/shard_map/while/body/eval_jaxpr/ppermute | solution.py:15
  275.1 9.0 %collective-permute-start = (f32[64,512]{1,0:T(8,128)S(1)}, f32[64,512]{1,0:T(8,128)S(1)}, u32[]{:S(2)}, u32[]{:S(2)}) collective-permute-start(f32[64,512]{1,0:T(8,128)S(1)} %convolution_add_fusion.4), channel_id=1, source_target_pairs={{1,0},{2,1},{3,2},{4,3},{5,4},{6,5},{7,6},{8,7},{9,8},{10,9},{11,1... | collective-permute-start | bytes 393224 | tf_op jit(solution)/shard_map/while/body/eval_jaxpr/ppermute | solution.py:15
  284.8 9.2 %collective-permute-start = (f32[64,512]{1,0:T(8,128)S(1)}, f32[64,512]{1,0:T(8,128)S(1)}, u32[]{:S(2)}, u32[]{:S(2)}) collective-permute-start(f32[64,512]{1,0:T(8,128)S(1)} %convolution_add_fusion.4), channel_id=1, source_target_pairs={{1,0},{2,1},{3,2},{4,3},{5,4},{6,5},{7,6},{8,7},{9,8},{10,9},{11,1... | collective-permute-start | bytes 393224 | tf_op jit(solution)/shard_map/while/body/eval_jaxpr/ppermute | solution.py:15
  294.8 10.3 %collective-permute-start = (f32[64,512]{1,0:T(8,128)S(1)}, f32[64,512]{1,0:T(8,128)S(1)}, u32[]{:S(2)}, u32[]{:S(2)}) collective-permute-start(f32[64,512]{1,0:T(8,128)S(1)} %convolution_add_fusion.4), channel_id=1, source_target_pairs={{1,0},{2,1},{3,2},{4,3},{5,4},{6,5},{7,6},{8,7},{9,8},{10,9},{11,1... | collective-permute-start | bytes 393224 | tf_op jit(solution)/shard_map/while/body/eval_jaxpr/ppermute | solution.py:15
  306.0 9.5 %collective-permute-start = (f32[64,512]{1,0:T(8,128)S(1)}, f32[64,512]{1,0:T(8,128)S(1)}, u32[]{:S(2)}, u32[]{:S(2)}) collective-permute-start(f32[64,512]{1,0:T(8,128)S(1)} %convolution_add_fusion.4), channel_id=1, source_target_pairs={{1,0},{2,1},{3,2},{4,3},{5,4},{6,5},{7,6},{8,7},{9,8},{10,9},{11,1... | collective-permute-start | bytes 393224 | tf_op jit(solution)/shard_map/while/body/eval_jaxpr/ppermute | solution.py:15
  316.2 9.0 %collective-permute-start = (f32[64,512]{1,0:T(8,128)S(1)}, f32[64,512]{1,0:T(8,128)S(1)}, u32[]{:S(2)}, u32[]{:S(2)}) collective-permute-start(f32[64,512]{1,0:T(8,128)S(1)} %convolution_add_fusion.4), channel_id=1, source_target_pairs={{1,0},{2,1},{3,2},{4,3},{5,4},{6,5},{7,6},{8,7},{9,8},{10,9},{11,1... | collective-permute-start | bytes 393224 | tf_op jit(solution)/shard_map/while/body/eval_jaxpr/ppermute | solution.py:15
  326.0 9.0 %collective-permute-start = (f32[64,512]{1,0:T(8,128)S(1)}, f32[64,512]{1,0:T(8,128)S(1)}, u32[]{:S(2)}, u32[]{:S(2)}) collective-permute-start(f32[64,512]{1,0:T(8,128)S(1)} %convolution_add_fusion.4), channel_id=1, source_target_pairs={{1,0},{2,1},{3,2},{4,3},{5,4},{6,5},{7,6},{8,7},{9,8},{10,9},{11,1... | collective-permute-start | bytes 393224 | tf_op jit(solution)/shard_map/while/body/eval_jaxpr/ppermute | solution.py:15
  335.8 9.0 %collective-permute-start = (f32[64,512]{1,0:T(8,128)S(1)}, f32[64,512]{1,0:T(8,128)S(1)}, u32[]{:S(2)}, u32[]{:S(2)}) collective-permute-start(f32[64,512]{1,0:T(8,128)S(1)} %convolution_add_fusion.4), channel_id=1, source_target_pairs={{1,0},{2,1},{3,2},{4,3},{5,4},{6,5},{7,6},{8,7},{9,8},{10,9},{11,1... | collective-permute-start | bytes 393224 | tf_op jit(solution)/shard_map/while/body/eval_jaxpr/ppermute | solution.py:15
  345.5 9.0 %collective-permute-start = (f32[64,512]{1,0:T(8,128)S(1)}, f32[64,512]{1,0:T(8,128)S(1)}, u32[]{:S(2)}, u32[]{:S(2)}) collective-permute-start(f32[64,512]{1,0:T(8,128)S(1)} %convolution_add_fusion.4), channel_id=1, source_target_pairs={{1,0},{2,1},{3,2},{4,3},{5,4},{6,5},{7,6},{8,7},{9,8},{10,9},{11,1... | collective-permute-start | bytes 393224 | tf_op jit(solution)/shard_map/while/body/eval_jaxpr/ppermute | solution.py:15
  355.3 9.0 %collective-permute-start = (f32[64,512]{1,0:T(8,128)S(1)}, f32[64,512]{1,0:T(8,128)S(1)}, u32[]{:S(2)}, u32[]{:S(2)}) collective-permute-start(f32[64,512]{1,0:T(8,128)S(1)} %convolution_add_fusion.4), channel_id=1, source_target_pairs={{1,0},{2,1},{3,2},{4,3},{5,4},{6,5},{7,6},{8,7},{9,8},{10,9},{11,1... | collective-permute-start | bytes 393224 | tf_op jit(solution)/shard_map/while/body/eval_jaxpr/ppermute | solution.py:15
  365.0 9.2 %collective-permute-start = (f32[64,512]{1,0:T(8,128)S(1)}, f32[64,512]{1,0:T(8,128)S(1)}, u32[]{:S(2)}, u32[]{:S(2)}) collective-permute-start(f32[64,512]{1,0:T(8,128)S(1)} %convolution_add_fusion.4), channel_id=1, source_target_pairs={{1,0},{2,1},{3,2},{4,3},{5,4},{6,5},{7,6},{8,7},{9,8},{10,9},{11,1... | collective-permute-start | bytes 393224 | tf_op jit(solution)/shard_map/while/body/eval_jaxpr/ppermute | solution.py:15
  375.1 10.4 %collective-permute-start = (f32[64,512]{1,0:T(8,128)S(1)}, f32[64,512]{1,0:T(8,128)S(1)}, u32[]{:S(2)}, u32[]{:S(2)}) collective-permute-start(f32[64,512]{1,0:T(8,128)S(1)} %convolution_add_fusion.4), channel_id=1, source_target_pairs={{1,0},{2,1},{3,2},{4,3},{5,4},{6,5},{7,6},{8,7},{9,8},{10,9},{11,1... | collective-permute-start | bytes 393224 | tf_op jit(solution)/shard_map/while/body/eval_jaxpr/ppermute | solution.py:15
  386.2 9.4 %collective-permute-start = (f32[64,512]{1,0:T(8,128)S(1)}, f32[64,512]{1,0:T(8,128)S(1)}, u32[]{:S(2)}, u32[]{:S(2)}) collective-permute-start(f32[64,512]{1,0:T(8,128)S(1)} %convolution_add_fusion.4), channel_id=1, source_target_pairs={{1,0},{2,1},{3,2},{4,3},{5,4},{6,5},{7,6},{8,7},{9,8},{10,9},{11,1... | collective-permute-start | bytes 393224 | tf_op jit(solution)/shard_map/while/body/eval_jaxpr/ppermute | solution.py:15
  396.4 9.0 %collective-permute-start = (f32[64,512]{1,0:T(8,128)S(1)}, f32[64,512]{1,0:T(8,128)S(1)}, u32[]{:S(2)}, u32[]{:S(2)}) collective-permute-start(f32[64,512]{1,0:T(8,128)S(1)} %convolution_add_fusion.4), channel_id=1, source_target_pairs={{1,0},{2,1},{3,2},{4,3},{5,4},{6,5},{7,6},{8,7},{9,8},{10,9},{11,1... | collective-permute-start | bytes 393224 | tf_op jit(solution)/shard_map/while/body/eval_jaxpr/ppermute | solution.py:15
  406.2 9.0 %collective-permute-start = (f32[64,512]{1,0:T(8,128)S(1)}, f32[64,512]{1,0:T(8,128)S(1)}, u32[]{:S(2)}, u32[]{:S(2)}) collective-permute-start(f32[64,512]{1,0:T(8,128)S(1)} %convolution_add_fusion.4), channel_id=1, source_target_pairs={{1,0},{2,1},{3,2},{4,3},{5,4},{6,5},{7,6},{8,7},{9,8},{10,9},{11,1... | collective-permute-start | bytes 393224 | tf_op jit(solution)/shard_map/while/body/eval_jaxpr/ppermute | solution.py:15
  416.0 9.0 %collective-permute-start = (f32[64,512]{1,0:T(8,128)S(1)}, f32[64,512]{1,0:T(8,128)S(1)}, u32[]{:S(2)}, u32[]{:S(2)}) collective-permute-start(f32[64,512]{1,0:T(8,128)S(1)} %convolution_add_fusion.4), channel_id=1, source_target_pairs={{1,0},{2,1},{3,2},{4,3},{5,4},{6,5},{7,6},{8,7},{9,8},{10,9},{11,1... | collective-permute-start | bytes 393224 | tf_op jit(solution)/shard_map/while/body/eval_jaxpr/ppermute | solution.py:15
  425.8 9.0 %collective-permute-start = (f32[64,512]{1,0:T(8,128)S(1)}, f32[64,512]{1,0:T(8,128)S(1)}, u32[]{:S(2)}, u32[]{:S(2)}) collective-permute-start(f32[64,512]{1,0:T(8,128)S(1)} %convolution_add_fusion.4), channel_id=1, source_target_pairs={{1,0},{2,1},{3,2},{4,3},{5,4},{6,5},{7,6},{8,7},{9,8},{10,9},{11,1... | collective-permute-start | bytes 393224 | tf_op jit(solution)/shard_map/while/body/eval_jaxpr/ppermute | solution.py:15
  435.5 9.0 %collective-permute-start = (f32[64,512]{1,0:T(8,128)S(1)}, f32[64,512]{1,0:T(8,128)S(1)}, u32[]{:S(2)}, u32[]{:S(2)}) collective-permute-start(f32[64,512]{1,0:T(8,128)S(1)} %convolution_add_fusion.4), channel_id=1, source_target_pairs={{1,0},{2,1},{3,2},{4,3},{5,4},{6,5},{7,6},{8,7},{9,8},{10,9},{11,1... | collective-permute-start | bytes 393224 | tf_op jit(solution)/shard_map/while/body/eval_jaxpr/ppermute | solution.py:15
Sparse Core Ops, SparseCore 0:
  10.9 119.8 all-reduce.1
where the time goes:
time: 456 us; the launch traced here: 455 us
  waiting for transfers between devices  206 us (45%)
  starting transfers between devices  200 us (44%)
  matrix products  31.3 us (7%)
  between operations  14.1 us (3%)
    ppermute x31, starting transfers between devices, from_behind(): return lax.ppermute(block, axis, route)  200 us
    psum x1, waiting for transfers between devices, shards(): landmark = lax.psum(partial_value, 'team')  120 us
    ppermute x31, waiting for transfers between devices, from_behind(): return lax.ppermute(block, axis, route)  85.5 us
    dot_general x33, matrix products, matmul(): return jnp.dot(left, right, precision=HIGHEST)  25.5 us
  transfers between devices with their start and end apart: 32, of which 32 were waited for; matrix products, arithmetic and copies ran while one was open for 0% of the time, Pallas kernels for 0%

commit v1 on v0

--- a/solution.py
+++ b/solution.py
@@ -24,7 +24,11 @@
     matrices = transitions[0]
     incident = incidence[0].astype(jnp.float32)
     partial_value = jnp.einsum("scr,srl->scl", measured[0], incident, precision=HIGHEST)
-    landmark = lax.psum(partial_value, "team")
+    landmark = partial_value
+    for hop in (1, 2, 4, 8):
+        landmark = landmark + lax.ppermute(
+            landmark, "team", [(dev, dev ^ hop) for dev in range(16)]
+        )
     injection = jnp.einsum("scl,srl->scr", landmark, incident, precision=HIGHEST)
     driven = cotangent[0] + jnp.repeat(injection, STATES, axis=2) * obs_gain[0][None, None, :]
     offset = jnp.zeros((COLS, TEAM_STATES), jnp.float32)

time: 456 us -> 401 us (0.88)
  the two profiles are of different devices: /device:TPU:30 before, /device:TPU:6 now
where the time goes in v1:
time: 401 us; the launch traced here: 400 us
  starting transfers between devices  223 us (56%)
  waiting for transfers between devices  144 us (36%)
  matrix products  29.5 us (7%)
    ppermute x31, starting transfers between devices, from_behind(): return lax.ppermute(block, axis, route)  205 us
    ppermute x31, waiting for transfers between devices, from_behind(): return lax.ppermute(block, axis, route)  83.5 us
    ppermute x4, waiting for transfers between devices, shards(): lax.ppermute(landmark, 'team', [(dev, dev ^ hop) for dev in range(16)])  60.2 us
    dot_general x33, matrix products, matmul(): return jnp.dot(left, right, precision=HIGHEST)  25.5 us
    ppermute x4, starting transfers between devices, shards(): lax.ppermute(landmark, 'team', [(dev, dev ^ hop) for dev in range(16)])  17.8 us
  transfers between devices with their start and end apart: 35, of which 35 were waited for; matrix products, arithmetic and copies ran while one was open for 0% of the time, Pallas kernels for 0%

profile of v1, /device:TPU:6, one launch (start us, length us, event | category | flops | bytes accessed | tf_op | source)
XLA Modules:
  0.0 399.6 jit_solution(7567412361982550878)
XLA Ops:
  6.1 3.5 collective-permute-start.2
  9.6 12.4 %collective-permute-done.2 = f32[1,64,2048]{2,1,0:T(8,128)S(1)} collective-permute-done((f32[1,64,2048]{2,1,0:T(8,128)S(1)}, f32[1,64,2048]{2,1,0:T(8,128)S(1)}, u32[]{:S(2)}, u32[]{:S(2)}) %collective-permute-start.2) | collective-permute-done | bytes 524320 | tf_op jit(solution)/shard_map/ppermute | solution.py:29
  22.1 4.6 %collective-permute-start.3 = (f32[1,64,2048]{2,1,0:T(8,128)S(1)}, f32[1,64,2048]{2,1,0:T(8,128)S(1)}, u32[]{:S(2)}, u32[]{:S(2)}) collective-permute-start(f32[1,64,2048]{2,1,0:T(8,128)S(1)} %add.34), channel_id=1, source_target_pairs={{0,128},{32,160},{64,192},{96,224},{128,0},{160,32},{192,64},{224,... | collective-permute-start | bytes 1572872 | tf_op jit(solution)/shard_map/ppermute | solution.py:29
  26.7 22.6 %collective-permute-done.3 = f32[1,64,2048]{2,1,0:T(8,128)S(1)} collective-permute-done((f32[1,64,2048]{2,1,0:T(8,128)S(1)}, f32[1,64,2048]{2,1,0:T(8,128)S(1)}, u32[]{:S(2)}, u32[]{:S(2)}) %collective-permute-start.3) | collective-permute-done | bytes 524320 | tf_op jit(solution)/shard_map/ppermute | solution.py:29
  49.4 7.7 %collective-permute-start.4 = (f32[1,64,2048]{2,1,0:T(8,128)S(1)}, f32[1,64,2048]{2,1,0:T(8,128)S(1)}, u32[]{:S(2)}, u32[]{:S(2)}) collective-permute-start(f32[1,64,2048]{2,1,0:T(8,128)S(1)} %add.35), channel_id=1, source_target_pairs={{0,256},{32,288},{64,320},{96,352},{128,384},{160,416},{192,448},{... | collective-permute-start | bytes 1572872 | tf_op jit(solution)/shard_map/ppermute | solution.py:29
  57.2 23.3 %collective-permute-done.4 = f32[1,64,2048]{2,1,0:T(8,128)S(1)} collective-permute-done((f32[1,64,2048]{2,1,0:T(8,128)S(1)}, f32[1,64,2048]{2,1,0:T(8,128)S(1)}, u32[]{:S(2)}, u32[]{:S(2)}) %collective-permute-start.4) | collective-permute-done | bytes 524320 | tf_op jit(solution)/shard_map/ppermute | solution.py:29
  82.8 313.6 %while.10 = (s32[]{:T(128)}, f32[64,512]{1,0:T(8,128)S(1)}, f32[1,1,512,512]{3,2,1,0:T(8,128)S(1)}, f32[64,512]{1,0:T(8,128)S(1)}, f32[64,512]{1,0:T(8,128)S(1)}, /*index=5*/s32[]{:T(128)}) while((s32[]{:T(128)}, f32[64,512]{1,0:T(8,128)S(1)}, f32[1,1,512,512]{3,2,1,0:T(8,128)S(1)}, f32[64,512]{1,0:T(8,128)S(1)}, f32[64,512]{1,0:T(8,128)S(1)}, ...), condition=%wide.region_1.2_spmd, body=%wide.region_0.1_spmd.sunk | while | flops 201392128 | bytes 2359405 | solution.py:46
  83.5 11.2 %collective-permute-start = (f32[64,512]{1,0:T(8,128)S(1)}, f32[64,512]{1,0:T(8,128)S(1)}, u32[]{:S(2)}, u32[]{:S(2)}) collective-permute-start(f32[64,512]{1,0:T(8,128)S(1)} %convolution_add_fusion.4), channel_id=1, source_target_pairs={{1,0},{2,1},{3,2},{4,3},{5,4},{6,5},{7,6},{8,7},{9,8},{10,9},{11,1... | collective-permute-start | bytes 393224 | tf_op jit(solution)/shard_map/while/body/eval_jaxpr/ppermute | solution.py:15
  94.7 2.5 collective-permute-done
  98.0 6.5 %collective-permute-start = (f32[64,512]{1,0:T(8,128)S(1)}, f32[64,512]{1,0:T(8,128)S(1)}, u32[]{:S(2)}, u32[]{:S(2)}) collective-permute-start(f32[64,512]{1,0:T(8,128)S(1)} %convolution_add_fusion.4), channel_id=1, source_target_pairs={{1,0},{2,1},{3,2},{4,3},{5,4},{6,5},{7,6},{8,7},{9,8},{10,9},{11,1... | collective-permute-start | bytes 393224 | tf_op jit(solution)/shard_map/while/body/eval_jaxpr/ppermute | solution.py:15
  107.8 6.5 %collective-permute-start = (f32[64,512]{1,0:T(8,128)S(1)}, f32[64,512]{1,0:T(8,128)S(1)}, u32[]{:S(2)}, u32[]{:S(2)}) collective-permute-start(f32[64,512]{1,0:T(8,128)S(1)} %convolution_add_fusion.4), channel_id=1, source_target_pairs={{1,0},{2,1},{3,2},{4,3},{5,4},{6,5},{7,6},{8,7},{9,8},{10,9},{11,1... | collective-permute-start | bytes 393224 | tf_op jit(solution)/shard_map/while/body/eval_jaxpr/ppermute | solution.py:15
  117.6 6.5 %collective-permute-start = (f32[64,512]{1,0:T(8,128)S(1)}, f32[64,512]{1,0:T(8,128)S(1)}, u32[]{:S(2)}, u32[]{:S(2)}) collective-permute-start(f32[64,512]{1,0:T(8,128)S(1)} %convolution_add_fusion.4), channel_id=1, source_target_pairs={{1,0},{2,1},{3,2},{4,3},{5,4},{6,5},{7,6},{8,7},{9,8},{10,9},{11,1... | collective-permute-start | bytes 393224 | tf_op jit(solution)/shard_map/while/body/eval_jaxpr/ppermute | solution.py:15
  127.3 6.5 %collective-permute-start = (f32[64,512]{1,0:T(8,128)S(1)}, f32[64,512]{1,0:T(8,128)S(1)}, u32[]{:S(2)}, u32[]{:S(2)}) collective-permute-start(f32[64,512]{1,0:T(8,128)S(1)} %convolution_add_fusion.4), channel_id=1, source_target_pairs={{1,0},{2,1},{3,2},{4,3},{5,4},{6,5},{7,6},{8,7},{9,8},{10,9},{11,1... | collective-permute-start | bytes 393224 | tf_op jit(solution)/shard_map/while/body/eval_jaxpr/ppermute | solution.py:15
  137.1 6.5 %collective-permute-start = (f32[64,512]{1,0:T(8,128)S(1)}, f32[64,512]{1,0:T(8,128)S(1)}, u32[]{:S(2)}, u32[]{:S(2)}) collective-permute-start(f32[64,512]{1,0:T(8,128)S(1)} %convolution_add_fusion.4), channel_id=1, source_target_pairs={{1,0},{2,1},{3,2},{4,3},{5,4},{6,5},{7,6},{8,7},{9,8},{10,9},{11,1... | collective-permute-start | bytes 393224 | tf_op jit(solution)/shard_map/while/body/eval_jaxpr/ppermute | solution.py:15
  143.5 2.8 collective-permute-done
  147.1 6.5 %collective-permute-start = (f32[64,512]{1,0:T(8,128)S(1)}, f32[64,512]{1,0:T(8,128)S(1)}, u32[]{:S(2)}, u32[]{:S(2)}) collective-permute-start(f32[64,512]{1,0:T(8,128)S(1)} %convolution_add_fusion.4), channel_id=1, source_target_pairs={{1,0},{2,1},{3,2},{4,3},{5,4},{6,5},{7,6},{8,7},{9,8},{10,9},{11,1... | collective-permute-start | bytes 393224 | tf_op jit(solution)/shard_map/while/body/eval_jaxpr/ppermute | solution.py:15
  153.6 3.8 collective-permute-done
  158.2 6.5 %collective-permute-start = (f32[64,512]{1,0:T(8,128)S(1)}, f32[64,512]{1,0:T(8,128)S(1)}, u32[]{:S(2)}, u32[]{:S(2)}) collective-permute-start(f32[64,512]{1,0:T(8,128)S(1)} %convolution_add_fusion.4), channel_id=1, source_target_pairs={{1,0},{2,1},{3,2},{4,3},{5,4},{6,5},{7,6},{8,7},{9,8},{10,9},{11,1... | collective-permute-start | bytes 393224 | tf_op jit(solution)/shard_map/while/body/eval_jaxpr/ppermute | solution.py:15
  164.7 2.9 collective-permute-done
  168.4 6.5 %collective-permute-start = (f32[64,512]{1,0:T(8,128)S(1)}, f32[64,512]{1,0:T(8,128)S(1)}, u32[]{:S(2)}, u32[]{:S(2)}) collective-permute-start(f32[64,512]{1,0:T(8,128)S(1)} %convolution_add_fusion.4), channel_id=1, source_target_pairs={{1,0},{2,1},{3,2},{4,3},{5,4},{6,5},{7,6},{8,7},{9,8},{10,9},{11,1... | collective-permute-start | bytes 393224 | tf_op jit(solution)/shard_map/while/body/eval_jaxpr/ppermute | solution.py:15
  178.2 6.5 %collective-permute-start = (f32[64,512]{1,0:T(8,128)S(1)}, f32[64,512]{1,0:T(8,128)S(1)}, u32[]{:S(2)}, u32[]{:S(2)}) collective-permute-start(f32[64,512]{1,0:T(8,128)S(1)} %convolution_add_fusion.4), channel_id=1, source_target_pairs={{1,0},{2,1},{3,2},{4,3},{5,4},{6,5},{7,6},{8,7},{9,8},{10,9},{11,1... | collective-permute-start | bytes 393224 | tf_op jit(solution)/shard_map/while/body/eval_jaxpr/ppermute | solution.py:15
  188.0 6.5 %collective-permute-start = (f32[64,512]{1,0:T(8,128)S(1)}, f32[64,512]{1,0:T(8,128)S(1)}, u32[]{:S(2)}, u32[]{:S(2)}) collective-permute-start(f32[64,512]{1,0:T(8,128)S(1)} %convolution_add_fusion.4), channel_id=1, source_target_pairs={{1,0},{2,1},{3,2},{4,3},{5,4},{6,5},{7,6},{8,7},{9,8},{10,9},{11,1... | collective-permute-start | bytes 393224 | tf_op jit(solution)/shard_map/while/body/eval_jaxpr/ppermute | solution.py:15
  197.7 6.5 %collective-permute-start = (f32[64,512]{1,0:T(8,128)S(1)}, f32[64,512]{1,0:T(8,128)S(1)}, u32[]{:S(2)}, u32[]{:S(2)}) collective-permute-start(f32[64,512]{1,0:T(8,128)S(1)} %convolution_add_fusion.4), channel_id=1, source_target_pairs={{1,0},{2,1},{3,2},{4,3},{5,4},{6,5},{7,6},{8,7},{9,8},{10,9},{11,1... | collective-permute-start | bytes 393224 | tf_op jit(solution)/shard_map/while/body/eval_jaxpr/ppermute | solution.py:15
  207.5 6.5 %collective-permute-start = (f32[64,512]{1,0:T(8,128)S(1)}, f32[64,512]{1,0:T(8,128)S(1)}, u32[]{:S(2)}, u32[]{:S(2)}) collective-permute-start(f32[64,512]{1,0:T(8,128)S(1)} %convolution_add_fusion.4), channel_id=1, source_target_pairs={{1,0},{2,1},{3,2},{4,3},{5,4},{6,5},{7,6},{8,7},{9,8},{10,9},{11,1... | collective-permute-start | bytes 393224 | tf_op jit(solution)/shard_map/while/body/eval_jaxpr/ppermute | solution.py:15
  217.3 6.5 %collective-permute-start = (f32[64,512]{1,0:T(8,128)S(1)}, f32[64,512]{1,0:T(8,128)S(1)}, u32[]{:S(2)}, u32[]{:S(2)}) collective-permute-start(f32[64,512]{1,0:T(8,128)S(1)} %convolution_add_fusion.4), channel_id=1, source_target_pairs={{1,0},{2,1},{3,2},{4,3},{5,4},{6,5},{7,6},{8,7},{9,8},{10,9},{11,1... | collective-permute-start | bytes 393224 | tf_op jit(solution)/shard_map/while/body/eval_jaxpr/ppermute | solution.py:15
  223.7 2.8 collective-permute-done
  227.3 6.5 %collective-permute-start = (f32[64,512]{1,0:T(8,128)S(1)}, f32[64,512]{1,0:T(8,128)S(1)}, u32[]{:S(2)}, u32[]{:S(2)}) collective-permute-start(f32[64,512]{1,0:T(8,128)S(1)} %convolution_add_fusion.4), channel_id=1, source_target_pairs={{1,0},{2,1},{3,2},{4,3},{5,4},{6,5},{7,6},{8,7},{9,8},{10,9},{11,1... | collective-permute-start | bytes 393224 | tf_op jit(solution)/shard_map/while/body/eval_jaxpr/ppermute | solution.py:15
  233.8 3.8 collective-permute-done
  238.4 6.5 %collective-permute-start = (f32[64,512]{1,0:T(8,128)S(1)}, f32[64,512]{1,0:T(8,128)S(1)}, u32[]{:S(2)}, u32[]{:S(2)}) collective-permute-start(f32[64,512]{1,0:T(8,128)S(1)} %convolution_add_fusion.4), channel_id=1, source_target_pairs={{1,0},{2,1},{3,2},{4,3},{5,4},{6,5},{7,6},{8,7},{9,8},{10,9},{11,1... | collective-permute-start | bytes 393224 | tf_op jit(solution)/shard_map/while/body/eval_jaxpr/ppermute | solution.py:15
  244.9 2.9 collective-permute-done
  248.6 6.5 %collective-permute-start = (f32[64,512]{1,0:T(8,128)S(1)}, f32[64,512]{1,0:T(8,128)S(1)}, u32[]{:S(2)}, u32[]{:S(2)}) collective-permute-start(f32[64,512]{1,0:T(8,128)S(1)} %convolution_add_fusion.4), channel_id=1, source_target_pairs={{1,0},{2,1},{3,2},{4,3},{5,4},{6,5},{7,6},{8,7},{9,8},{10,9},{11,1... | collective-permute-start | bytes 393224 | tf_op jit(solution)/shard_map/while/body/eval_jaxpr/ppermute | solution.py:15
  258.4 6.5 %collective-permute-start = (f32[64,512]{1,0:T(8,128)S(1)}, f32[64,512]{1,0:T(8,128)S(1)}, u32[]{:S(2)}, u32[]{:S(2)}) collective-permute-start(f32[64,512]{1,0:T(8,128)S(1)} %convolution_add_fusion.4), channel_id=1, source_target_pairs={{1,0},{2,1},{3,2},{4,3},{5,4},{6,5},{7,6},{8,7},{9,8},{10,9},{11,1... | collective-permute-start | bytes 393224 | tf_op jit(solution)/shard_map/while/body/eval_jaxpr/ppermute | solution.py:15
  268.2 6.5 %collective-permute-start = (f32[64,512]{1,0:T(8,128)S(1)}, f32[64,512]{1,0:T(8,128)S(1)}, u32[]{:S(2)}, u32[]{:S(2)}) collective-permute-start(f32[64,512]{1,0:T(8,128)S(1)} %convolution_add_fusion.4), channel_id=1, source_target_pairs={{1,0},{2,1},{3,2},{4,3},{5,4},{6,5},{7,6},{8,7},{9,8},{10,9},{11,1... | collective-permute-start | bytes 393224 | tf_op jit(solution)/shard_map/while/body/eval_jaxpr/ppermute | solution.py:15
  277.9 6.5 %collective-permute-start = (f32[64,512]{1,0:T(8,128)S(1)}, f32[64,512]{1,0:T(8,128)S(1)}, u32[]{:S(2)}, u32[]{:S(2)}) collective-permute-start(f32[64,512]{1,0:T(8,128)S(1)} %convolution_add_fusion.4), channel_id=1, source_target_pairs={{1,0},{2,1},{3,2},{4,3},{5,4},{6,5},{7,6},{8,7},{9,8},{10,9},{11,1... | collective-permute-start | bytes 393224 | tf_op jit(solution)/shard_map/while/body/eval_jaxpr/ppermute | solution.py:15
  287.7 6.5 %collective-permute-start = (f32[64,512]{1,0:T(8,128)S(1)}, f32[64,512]{1,0:T(8,128)S(1)}, u32[]{:S(2)}, u32[]{:S(2)}) collective-permute-start(f32[64,512]{1,0:T(8,128)S(1)} %convolution_add_fusion.4), channel_id=1, source_target_pairs={{1,0},{2,1},{3,2},{4,3},{5,4},{6,5},{7,6},{8,7},{9,8},{10,9},{11,1... | collective-permute-start | bytes 393224 | tf_op jit(solution)/shard_map/while/body/eval_jaxpr/ppermute | solution.py:15
  297.4 6.5 %collective-permute-start = (f32[64,512]{1,0:T(8,128)S(1)}, f32[64,512]{1,0:T(8,128)S(1)}, u32[]{:S(2)}, u32[]{:S(2)}) collective-permute-start(f32[64,512]{1,0:T(8,128)S(1)} %convolution_add_fusion.4), channel_id=1, source_target_pairs={{1,0},{2,1},{3,2},{4,3},{5,4},{6,5},{7,6},{8,7},{9,8},{10,9},{11,1... | collective-permute-start | bytes 393224 | tf_op jit(solution)/shard_map/while/body/eval_jaxpr/ppermute | solution.py:15
  303.9 2.8 collective-permute-done
  307.5 6.5 %collective-permute-start = (f32[64,512]{1,0:T(8,128)S(1)}, f32[64,512]{1,0:T(8,128)S(1)}, u32[]{:S(2)}, u32[]{:S(2)}) collective-permute-start(f32[64,512]{1,0:T(8,128)S(1)} %convolution_add_fusion.4), channel_id=1, source_target_pairs={{1,0},{2,1},{3,2},{4,3},{5,4},{6,5},{7,6},{8,7},{9,8},{10,9},{11,1... | collective-permute-start | bytes 393224 | tf_op jit(solution)/shard_map/while/body/eval_jaxpr/ppermute | solution.py:15
  314.0 3.8 collective-permute-done
  318.6 6.5 %collective-permute-start = (f32[64,512]{1,0:T(8,128)S(1)}, f32[64,512]{1,0:T(8,128)S(1)}, u32[]{:S(2)}, u32[]{:S(2)}) collective-permute-start(f32[64,512]{1,0:T(8,128)S(1)} %convolution_add_fusion.4), channel_id=1, source_target_pairs={{1,0},{2,1},{3,2},{4,3},{5,4},{6,5},{7,6},{8,7},{9,8},{10,9},{11,1... | collective-permute-start | bytes 393224 | tf_op jit(solution)/shard_map/while/body/eval_jaxpr/ppermute | solution.py:15
  325.1 2.9 collective-permute-done
  328.8 6.5 %collective-permute-start = (f32[64,512]{1,0:T(8,128)S(1)}, f32[64,512]{1,0:T(8,128)S(1)}, u32[]{:S(2)}, u32[]{:S(2)}) collective-permute-start(f32[64,512]{1,0:T(8,128)S(1)} %convolution_add_fusion.4), channel_id=1, source_target_pairs={{1,0},{2,1},{3,2},{4,3},{5,4},{6,5},{7,6},{8,7},{9,8},{10,9},{11,1... | collective-permute-start | bytes 393224 | tf_op jit(solution)/shard_map/while/body/eval_jaxpr/ppermute | solution.py:15
  338.6 6.5 %collective-permute-start = (f32[64,512]{1,0:T(8,128)S(1)}, f32[64,512]{1,0:T(8,128)S(1)}, u32[]{:S(2)}, u32[]{:S(2)}) collective-permute-start(f32[64,512]{1,0:T(8,128)S(1)} %convolution_add_fusion.4), channel_id=1, source_target_pairs={{1,0},{2,1},{3,2},{4,3},{5,4},{6,5},{7,6},{8,7},{9,8},{10,9},{11,1... | collective-permute-start | bytes 393224 | tf_op jit(solution)/shard_map/while/body/eval_jaxpr/ppermute | solution.py:15
  348.4 6.5 %collective-permute-start = (f32[64,512]{1,0:T(8,128)S(1)}, f32[64,512]{1,0:T(8,128)S(1)}, u32[]{:S(2)}, u32[]{:S(2)}) collective-permute-start(f32[64,512]{1,0:T(8,128)S(1)} %convolution_add_fusion.4), channel_id=1, source_target_pairs={{1,0},{2,1},{3,2},{4,3},{5,4},{6,5},{7,6},{8,7},{9,8},{10,9},{11,1... | collective-permute-start | bytes 393224 | tf_op jit(solution)/shard_map/while/body/eval_jaxpr/ppermute | solution.py:15
  358.1 6.5 %collective-permute-start = (f32[64,512]{1,0:T(8,128)S(1)}, f32[64,512]{1,0:T(8,128)S(1)}, u32[]{:S(2)}, u32[]{:S(2)}) collective-permute-start(f32[64,512]{1,0:T(8,128)S(1)} %convolution_add_fusion.4), channel_id=1, source_target_pairs={{1,0},{2,1},{3,2},{4,3},{5,4},{6,5},{7,6},{8,7},{9,8},{10,9},{11,1... | collective-permute-start | bytes 393224 | tf_op jit(solution)/shard_map/while/body/eval_jaxpr/ppermute | solution.py:15
  367.9 6.5 %collective-permute-start = (f32[64,512]{1,0:T(8,128)S(1)}, f32[64,512]{1,0:T(8,128)S(1)}, u32[]{:S(2)}, u32[]{:S(2)}) collective-permute-start(f32[64,512]{1,0:T(8,128)S(1)} %convolution_add_fusion.4), channel_id=1, source_target_pairs={{1,0},{2,1},{3,2},{4,3},{5,4},{6,5},{7,6},{8,7},{9,8},{10,9},{11,1... | collective-permute-start | bytes 393224 | tf_op jit(solution)/shard_map/while/body/eval_jaxpr/ppermute | solution.py:15
  377.6 6.5 %collective-permute-start = (f32[64,512]{1,0:T(8,128)S(1)}, f32[64,512]{1,0:T(8,128)S(1)}, u32[]{:S(2)}, u32[]{:S(2)}) collective-permute-start(f32[64,512]{1,0:T(8,128)S(1)} %convolution_add_fusion.4), channel_id=1, source_target_pairs={{1,0},{2,1},{3,2},{4,3},{5,4},{6,5},{7,6},{8,7},{9,8},{10,9},{11,1... | collective-permute-start | bytes 393224 | tf_op jit(solution)/shard_map/while/body/eval_jaxpr/ppermute | solution.py:15
  387.4 6.5 %collective-permute-start = (f32[64,512]{1,0:T(8,128)S(1)}, f32[64,512]{1,0:T(8,128)S(1)}, u32[]{:S(2)}, u32[]{:S(2)}) collective-permute-start(f32[64,512]{1,0:T(8,128)S(1)} %convolution_add_fusion.4), channel_id=1, source_target_pairs={{1,0},{2,1},{3,2},{4,3},{5,4},{6,5},{7,6},{8,7},{9,8},{10,9},{11,1... | collective-permute-start | bytes 393224 | tf_op jit(solution)/shard_map/while/body/eval_jaxpr/ppermute | solution.py:15
  (109 shorter events, 87.5 us)
Async XLA Ops:
  0.6 397.2 %copy-start = (f32[1,1,64,512]{3,2,1,0:T(8,128)S(1)}, f32[1,1,64,512]{3,2,1,0:T(8,128)}, u32[]{:S(2)}) copy-start(f32[1,1,64,512]{3,2,1,0:T(8,128)} %param.10) | copy-start | bytes 393220
  2.3 3.8 collective-permute-start.1
  6.1 15.9 %collective-permute-start.2 = (f32[1,64,2048]{2,1,0:T(8,128)S(1)}, f32[1,64,2048]{2,1,0:T(8,128)S(1)}, u32[]{:S(2)}, u32[]{:S(2)}) collective-permute-start(f32[1,64,2048]{2,1,0:T(8,128)S(1)} %add.33), channel_id=1, source_target_pairs={{0,64},{32,96},{64,0},{96,32},{128,192},{160,224},{192,128},{224,1... | collective-permute-start | bytes 1572872 | tf_op jit(solution)/shard_map/ppermute | solution.py:29
  22.1 35.1 %copy-start.4 = (f32[1,64,512]{2,1,0:T(8,128)S(1)}, f32[1,64,512]{2,1,0:T(8,128)}, u32[]{:S(2)}) copy-start(f32[1,64,512]{2,1,0:T(8,128)} %param.12) | copy-start | bytes 393220
  22.1 27.3 %collective-permute-start.3 = (f32[1,64,2048]{2,1,0:T(8,128)S(1)}, f32[1,64,2048]{2,1,0:T(8,128)S(1)}, u32[]{:S(2)}, u32[]{:S(2)}) collective-permute-start(f32[1,64,2048]{2,1,0:T(8,128)S(1)} %add.34), channel_id=1, source_target_pairs={{0,128},{32,160},{64,192},{96,224},{128,0},{160,32},{192,64},{224,... | collective-permute-start | bytes 1572872 | tf_op jit(solution)/shard_map/ppermute | solution.py:29
  49.4 31.1 %collective-permute-start.4 = (f32[1,64,2048]{2,1,0:T(8,128)S(1)}, f32[1,64,2048]{2,1,0:T(8,128)S(1)}, u32[]{:S(2)}, u32[]{:S(2)}) collective-permute-start(f32[1,64,2048]{2,1,0:T(8,128)S(1)} %add.35), channel_id=1, source_target_pairs={{0,256},{32,288},{64,320},{96,352},{128,384},{160,416},{192,448},{... | collective-permute-start | bytes 1572872 | tf_op jit(solution)/shard_map/ppermute | solution.py:29
  57.2 23.4 %copy-start.2 = (s32[1,1,32,2048]{3,2,1,0:T(8,128)S(1)}, s32[1,1,32,2048]{3,2,1,0:T(8,128)}, u32[]{:S(2)}) copy-start(s32[1,1,32,2048]{3,2,1,0:T(8,128)} %param.13) | copy-start | bytes 786436
  57.2 24.0 %copy-start.1 = (f32[1,1,512,512]{3,2,1,0:T(8,128)S(1)}, f32[1,1,512,512]{3,2,1,0:T(8,128)}, u32[]{:S(2)}) copy-start(f32[1,1,512,512]{3,2,1,0:T(8,128)} %param.9) | copy-start | bytes 3145732
  81.1 0.9 copy-start.3
  81.1 0.9 copy-start.5
  83.5 13.7 %collective-permute-start = (f32[64,512]{1,0:T(8,128)S(1)}, f32[64,512]{1,0:T(8,128)S(1)}, u32[]{:S(2)}, u32[]{:S(2)}) collective-permute-start(f32[64,512]{1,0:T(8,128)S(1)} %convolution_add_fusion.4), channel_id=1, source_target_pairs={{1,0},{2,1},{3,2},{4,3},{5,4},{6,5},{7,6},{8,7},{9,8},{10,9},{11,1... | collective-permute-start | bytes 393224 | tf_op jit(solution)/shard_map/while/body/eval_jaxpr/ppermute | solution.py:15
  98.0 9.0 %collective-permute-start = (f32[64,512]{1,0:T(8,128)S(1)}, f32[64,512]{1,0:T(8,128)S(1)}, u32[]{:S(2)}, u32[]{:S(2)}) collective-permute-start(f32[64,512]{1,0:T(8,128)S(1)} %convolution_add_fusion.4), channel_id=1, source_target_pairs={{1,0},{2,1},{3,2},{4,3},{5,4},{6,5},{7,6},{8,7},{9,8},{10,9},{11,1... | collective-permute-start | bytes 393224 | tf_op jit(solution)/shard_map/while/body/eval_jaxpr/ppermute | solution.py:15
  107.8 9.0 %collective-permute-start = (f32[64,512]{1,0:T(8,128)S(1)}, f32[64,512]{1,0:T(8,128)S(1)}, u32[]{:S(2)}, u32[]{:S(2)}) collective-permute-start(f32[64,512]{1,0:T(8,128)S(1)} %convolution_add_fusion.4), channel_id=1, source_target_pairs={{1,0},{2,1},{3,2},{4,3},{5,4},{6,5},{7,6},{8,7},{9,8},{10,9},{11,1... | collective-permute-start | bytes 393224 | tf_op jit(solution)/shard_map/while/body/eval_jaxpr/ppermute | solution.py:15
  117.6 9.0 %collective-permute-start = (f32[64,512]{1,0:T(8,128)S(1)}, f32[64,512]{1,0:T(8,128)S(1)}, u32[]{:S(2)}, u32[]{:S(2)}) collective-permute-start(f32[64,512]{1,0:T(8,128)S(1)} %convolution_add_fusion.4), channel_id=1, source_target_pairs={{1,0},{2,1},{3,2},{4,3},{5,4},{6,5},{7,6},{8,7},{9,8},{10,9},{11,1... | collective-permute-start | bytes 393224 | tf_op jit(solution)/shard_map/while/body/eval_jaxpr/ppermute | solution.py:15
  127.3 9.0 %collective-permute-start = (f32[64,512]{1,0:T(8,128)S(1)}, f32[64,512]{1,0:T(8,128)S(1)}, u32[]{:S(2)}, u32[]{:S(2)}) collective-permute-start(f32[64,512]{1,0:T(8,128)S(1)} %convolution_add_fusion.4), channel_id=1, source_target_pairs={{1,0},{2,1},{3,2},{4,3},{5,4},{6,5},{7,6},{8,7},{9,8},{10,9},{11,1... | collective-permute-start | bytes 393224 | tf_op jit(solution)/shard_map/while/body/eval_jaxpr/ppermute | solution.py:15
  137.1 9.3 %collective-permute-start = (f32[64,512]{1,0:T(8,128)S(1)}, f32[64,512]{1,0:T(8,128)S(1)}, u32[]{:S(2)}, u32[]{:S(2)}) collective-permute-start(f32[64,512]{1,0:T(8,128)S(1)} %convolution_add_fusion.4), channel_id=1, source_target_pairs={{1,0},{2,1},{3,2},{4,3},{5,4},{6,5},{7,6},{8,7},{9,8},{10,9},{11,1... | collective-permute-start | bytes 393224 | tf_op jit(solution)/shard_map/while/body/eval_jaxpr/ppermute | solution.py:15
  147.1 10.3 %collective-permute-start = (f32[64,512]{1,0:T(8,128)S(1)}, f32[64,512]{1,0:T(8,128)S(1)}, u32[]{:S(2)}, u32[]{:S(2)}) collective-permute-start(f32[64,512]{1,0:T(8,128)S(1)} %convolution_add_fusion.4), channel_id=1, source_target_pairs={{1,0},{2,1},{3,2},{4,3},{5,4},{6,5},{7,6},{8,7},{9,8},{10,9},{11,1... | collective-permute-start | bytes 393224 | tf_op jit(solution)/shard_map/while/body/eval_jaxpr/ppermute | solution.py:15
  158.2 9.4 %collective-permute-start = (f32[64,512]{1,0:T(8,128)S(1)}, f32[64,512]{1,0:T(8,128)S(1)}, u32[]{:S(2)}, u32[]{:S(2)}) collective-permute-start(f32[64,512]{1,0:T(8,128)S(1)} %convolution_add_fusion.4), channel_id=1, source_target_pairs={{1,0},{2,1},{3,2},{4,3},{5,4},{6,5},{7,6},{8,7},{9,8},{10,9},{11,1... | collective-permute-start | bytes 393224 | tf_op jit(solution)/shard_map/while/body/eval_jaxpr/ppermute | solution.py:15
  168.4 9.0 %collective-permute-start = (f32[64,512]{1,0:T(8,128)S(1)}, f32[64,512]{1,0:T(8,128)S(1)}, u32[]{:S(2)}, u32[]{:S(2)}) collective-permute-start(f32[64,512]{1,0:T(8,128)S(1)} %convolution_add_fusion.4), channel_id=1, source_target_pairs={{1,0},{2,1},{3,2},{4,3},{5,4},{6,5},{7,6},{8,7},{9,8},{10,9},{11,1... | collective-permute-start | bytes 393224 | tf_op jit(solution)/shard_map/while/body/eval_jaxpr/ppermute | solution.py:15
  178.2 9.0 %collective-permute-start = (f32[64,512]{1,0:T(8,128)S(1)}, f32[64,512]{1,0:T(8,128)S(1)}, u32[]{:S(2)}, u32[]{:S(2)}) collective-permute-start(f32[64,512]{1,0:T(8,128)S(1)} %convolution_add_fusion.4), channel_id=1, source_target_pairs={{1,0},{2,1},{3,2},{4,3},{5,4},{6,5},{7,6},{8,7},{9,8},{10,9},{11,1... | collective-permute-start | bytes 393224 | tf_op jit(solution)/shard_map/while/body/eval_jaxpr/ppermute | solution.py:15
  188.0 9.0 %collective-permute-start = (f32[64,512]{1,0:T(8,128)S(1)}, f32[64,512]{1,0:T(8,128)S(1)}, u32[]{:S(2)}, u32[]{:S(2)}) collective-permute-start(f32[64,512]{1,0:T(8,128)S(1)} %convolution_add_fusion.4), channel_id=1, source_target_pairs={{1,0},{2,1},{3,2},{4,3},{5,4},{6,5},{7,6},{8,7},{9,8},{10,9},{11,1... | collective-permute-start | bytes 393224 | tf_op jit(solution)/shard_map/while/body/eval_jaxpr/ppermute | solution.py:15
  197.7 9.0 %collective-permute-start = (f32[64,512]{1,0:T(8,128)S(1)}, f32[64,512]{1,0:T(8,128)S(1)}, u32[]{:S(2)}, u32[]{:S(2)}) collective-permute-start(f32[64,512]{1,0:T(8,128)S(1)} %convolution_add_fusion.4), channel_id=1, source_target_pairs={{1,0},{2,1},{3,2},{4,3},{5,4},{6,5},{7,6},{8,7},{9,8},{10,9},{11,1... | collective-permute-start | bytes 393224 | tf_op jit(solution)/shard_map/while/body/eval_jaxpr/ppermute | solution.py:15
  207.5 9.0 %collective-permute-start = (f32[64,512]{1,0:T(8,128)S(1)}, f32[64,512]{1,0:T(8,128)S(1)}, u32[]{:S(2)}, u32[]{:S(2)}) collective-permute-start(f32[64,512]{1,0:T(8,128)S(1)} %convolution_add_fusion.4), channel_id=1, source_target_pairs={{1,0},{2,1},{3,2},{4,3},{5,4},{6,5},{7,6},{8,7},{9,8},{10,9},{11,1... | collective-permute-start | bytes 393224 | tf_op jit(solution)/shard_map/while/body/eval_jaxpr/ppermute | solution.py:15
  217.3 9.3 %collective-permute-start = (f32[64,512]{1,0:T(8,128)S(1)}, f32[64,512]{1,0:T(8,128)S(1)}, u32[]{:S(2)}, u32[]{:S(2)}) collective-permute-start(f32[64,512]{1,0:T(8,128)S(1)} %convolution_add_fusion.4), channel_id=1, source_target_pairs={{1,0},{2,1},{3,2},{4,3},{5,4},{6,5},{7,6},{8,7},{9,8},{10,9},{11,1... | collective-permute-start | bytes 393224 | tf_op jit(solution)/shard_map/while/body/eval_jaxpr/ppermute | solution.py:15
  227.3 10.3 %collective-permute-start = (f32[64,512]{1,0:T(8,128)S(1)}, f32[64,512]{1,0:T(8,128)S(1)}, u32[]{:S(2)}, u32[]{:S(2)}) collective-permute-start(f32[64,512]{1,0:T(8,128)S(1)} %convolution_add_fusion.4), channel_id=1, source_target_pairs={{1,0},{2,1},{3,2},{4,3},{5,4},{6,5},{7,6},{8,7},{9,8},{10,9},{11,1... | collective-permute-start | bytes 393224 | tf_op jit(solution)/shard_map/while/body/eval_jaxpr/ppermute | solution.py:15
  238.4 9.4 %collective-permute-start = (f32[64,512]{1,0:T(8,128)S(1)}, f32[64,512]{1,0:T(8,128)S(1)}, u32[]{:S(2)}, u32[]{:S(2)}) collective-permute-start(f32[64,512]{1,0:T(8,128)S(1)} %convolution_add_fusion.4), channel_id=1, source_target_pairs={{1,0},{2,1},{3,2},{4,3},{5,4},{6,5},{7,6},{8,7},{9,8},{10,9},{11,1... | collective-permute-start | bytes 393224 | tf_op jit(solution)/shard_map/while/body/eval_jaxpr/ppermute | solution.py:15
  248.6 9.0 %collective-permute-start = (f32[64,512]{1,0:T(8,128)S(1)}, f32[64,512]{1,0:T(8,128)S(1)}, u32[]{:S(2)}, u32[]{:S(2)}) collective-permute-start(f32[64,512]{1,0:T(8,128)S(1)} %convolution_add_fusion.4), channel_id=1, source_target_pairs={{1,0},{2,1},{3,2},{4,3},{5,4},{6,5},{7,6},{8,7},{9,8},{10,9},{11,1... | collective-permute-start | bytes 393224 | tf_op jit(solution)/shard_map/while/body/eval_jaxpr/ppermute | solution.py:15
  258.4 9.0 %collective-permute-start = (f32[64,512]{1,0:T(8,128)S(1)}, f32[64,512]{1,0:T(8,128)S(1)}, u32[]{:S(2)}, u32[]{:S(2)}) collective-permute-start(f32[64,512]{1,0:T(8,128)S(1)} %convolution_add_fusion.4), channel_id=1, source_target_pairs={{1,0},{2,1},{3,2},{4,3},{5,4},{6,5},{7,6},{8,7},{9,8},{10,9},{11,1... | collective-permute-start | bytes 393224 | tf_op jit(solution)/shard_map/while/body/eval_jaxpr/ppermute | solution.py:15
  268.2 9.0 %collective-permute-start = (f32[64,512]{1,0:T(8,128)S(1)}, f32[64,512]{1,0:T(8,128)S(1)}, u32[]{:S(2)}, u32[]{:S(2)}) collective-permute-start(f32[64,512]{1,0:T(8,128)S(1)} %convolution_add_fusion.4), channel_id=1, source_target_pairs={{1,0},{2,1},{3,2},{4,3},{5,4},{6,5},{7,6},{8,7},{9,8},{10,9},{11,1... | collective-permute-start | bytes 393224 | tf_op jit(solution)/shard_map/while/body/eval_jaxpr/ppermute | solution.py:15
  277.9 9.0 %collective-permute-start = (f32[64,512]{1,0:T(8,128)S(1)}, f32[64,512]{1,0:T(8,128)S(1)}, u32[]{:S(2)}, u32[]{:S(2)}) collective-permute-start(f32[64,512]{1,0:T(8,128)S(1)} %convolution_add_fusion.4), channel_id=1, source_target_pairs={{1,0},{2,1},{3,2},{4,3},{5,4},{6,5},{7,6},{8,7},{9,8},{10,9},{11,1... | collective-permute-start | bytes 393224 | tf_op jit(solution)/shard_map/while/body/eval_jaxpr/ppermute | solution.py:15
  287.7 9.0 %collective-permute-start = (f32[64,512]{1,0:T(8,128)S(1)}, f32[64,512]{1,0:T(8,128)S(1)}, u32[]{:S(2)}, u32[]{:S(2)}) collective-permute-start(f32[64,512]{1,0:T(8,128)S(1)} %convolution_add_fusion.4), channel_id=1, source_target_pairs={{1,0},{2,1},{3,2},{4,3},{5,4},{6,5},{7,6},{8,7},{9,8},{10,9},{11,1... | collective-permute-start | bytes 393224 | tf_op jit(solution)/shard_map/while/body/eval_jaxpr/ppermute | solution.py:15
  297.4 9.3 %collective-permute-start = (f32[64,512]{1,0:T(8,128)S(1)}, f32[64,512]{1,0:T(8,128)S(1)}, u32[]{:S(2)}, u32[]{:S(2)}) collective-permute-start(f32[64,512]{1,0:T(8,128)S(1)} %convolution_add_fusion.4), channel_id=1, source_target_pairs={{1,0},{2,1},{3,2},{4,3},{5,4},{6,5},{7,6},{8,7},{9,8},{10,9},{11,1... | collective-permute-start | bytes 393224 | tf_op jit(solution)/shard_map/while/body/eval_jaxpr/ppermute | solution.py:15
  307.5 10.3 %collective-permute-start = (f32[64,512]{1,0:T(8,128)S(1)}, f32[64,512]{1,0:T(8,128)S(1)}, u32[]{:S(2)}, u32[]{:S(2)}) collective-permute-start(f32[64,512]{1,0:T(8,128)S(1)} %convolution_add_fusion.4), channel_id=1, source_target_pairs={{1,0},{2,1},{3,2},{4,3},{5,4},{6,5},{7,6},{8,7},{9,8},{10,9},{11,1... | collective-permute-start | bytes 393224 | tf_op jit(solution)/shard_map/while/body/eval_jaxpr/ppermute | solution.py:15
  318.6 9.4 %collective-permute-start = (f32[64,512]{1,0:T(8,128)S(1)}, f32[64,512]{1,0:T(8,128)S(1)}, u32[]{:S(2)}, u32[]{:S(2)}) collective-permute-start(f32[64,512]{1,0:T(8,128)S(1)} %convolution_add_fusion.4), channel_id=1, source_target_pairs={{1,0},{2,1},{3,2},{4,3},{5,4},{6,5},{7,6},{8,7},{9,8},{10,9},{11,1... | collective-permute-start | bytes 393224 | tf_op jit(solution)/shard_map/while/body/eval_jaxpr/ppermute | solution.py:15
  328.8 9.0 %collective-permute-start = (f32[64,512]{1,0:T(8,128)S(1)}, f32[64,512]{1,0:T(8,128)S(1)}, u32[]{:S(2)}, u32[]{:S(2)}) collective-permute-start(f32[64,512]{1,0:T(8,128)S(1)} %convolution_add_fusion.4), channel_id=1, source_target_pairs={{1,0},{2,1},{3,2},{4,3},{5,4},{6,5},{7,6},{8,7},{9,8},{10,9},{11,1... | collective-permute-start | bytes 393224 | tf_op jit(solution)/shard_map/while/body/eval_jaxpr/ppermute | solution.py:15
  338.6 9.0 %collective-permute-start = (f32[64,512]{1,0:T(8,128)S(1)}, f32[64,512]{1,0:T(8,128)S(1)}, u32[]{:S(2)}, u32[]{:S(2)}) collective-permute-start(f32[64,512]{1,0:T(8,128)S(1)} %convolution_add_fusion.4), channel_id=1, source_target_pairs={{1,0},{2,1},{3,2},{4,3},{5,4},{6,5},{7,6},{8,7},{9,8},{10,9},{11,1... | collective-permute-start | bytes 393224 | tf_op jit(solution)/shard_map/while/body/eval_jaxpr/ppermute | solution.py:15
  348.4 9.0 %collective-permute-start = (f32[64,512]{1,0:T(8,128)S(1)}, f32[64,512]{1,0:T(8,128)S(1)}, u32[]{:S(2)}, u32[]{:S(2)}) collective-permute-start(f32[64,512]{1,0:T(8,128)S(1)} %convolution_add_fusion.4), channel_id=1, source_target_pairs={{1,0},{2,1},{3,2},{4,3},{5,4},{6,5},{7,6},{8,7},{9,8},{10,9},{11,1... | collective-permute-start | bytes 393224 | tf_op jit(solution)/shard_map/while/body/eval_jaxpr/ppermute | solution.py:15
  358.1 9.0 %collective-permute-start = (f32[64,512]{1,0:T(8,128)S(1)}, f32[64,512]{1,0:T(8,128)S(1)}, u32[]{:S(2)}, u32[]{:S(2)}) collective-permute-start(f32[64,512]{1,0:T(8,128)S(1)} %convolution_add_fusion.4), channel_id=1, source_target_pairs={{1,0},{2,1},{3,2},{4,3},{5,4},{6,5},{7,6},{8,7},{9,8},{10,9},{11,1... | collective-permute-start | bytes 393224 | tf_op jit(solution)/shard_map/while/body/eval_jaxpr/ppermute | solution.py:15
  367.9 9.0 %collective-permute-start = (f32[64,512]{1,0:T(8,128)S(1)}, f32[64,512]{1,0:T(8,128)S(1)}, u32[]{:S(2)}, u32[]{:S(2)}) collective-permute-start(f32[64,512]{1,0:T(8,128)S(1)} %convolution_add_fusion.4), channel_id=1, source_target_pairs={{1,0},{2,1},{3,2},{4,3},{5,4},{6,5},{7,6},{8,7},{9,8},{10,9},{11,1... | collective-permute-start | bytes 393224 | tf_op jit(solution)/shard_map/while/body/eval_jaxpr/ppermute | solution.py:15
  377.6 9.0 %collective-permute-start = (f32[64,512]{1,0:T(8,128)S(1)}, f32[64,512]{1,0:T(8,128)S(1)}, u32[]{:S(2)}, u32[]{:S(2)}) collective-permute-start(f32[64,512]{1,0:T(8,128)S(1)} %convolution_add_fusion.4), channel_id=1, source_target_pairs={{1,0},{2,1},{3,2},{4,3},{5,4},{6,5},{7,6},{8,7},{9,8},{10,9},{11,1... | collective-permute-start | bytes 393224 | tf_op jit(solution)/shard_map/while/body/eval_jaxpr/ppermute | solution.py:15
  387.4 9.0 %collective-permute-start = (f32[64,512]{1,0:T(8,128)S(1)}, f32[64,512]{1,0:T(8,128)S(1)}, u32[]{:S(2)}, u32[]{:S(2)}) collective-permute-start(f32[64,512]{1,0:T(8,128)S(1)} %convolution_add_fusion.4), channel_id=1, source_target_pairs={{1,0},{2,1},{3,2},{4,3},{5,4},{6,5},{7,6},{8,7},{9,8},{10,9},{11,1... | collective-permute-start | bytes 393224 | tf_op jit(solution)/shard_map/while/body/eval_jaxpr/ppermute | solution.py:15
